TPU v7x, 256 devices: a whole 4x4x8 slice. The times are simulated.
256 devices in a mesh: dp: 8 (over y, core), tensor: 32 (over x, z).
Axes of the slice: x: 4, y: 4, z: 8, core: 2. Of those that a mesh axis runs over, the one named last changes fastest.
Arguments:
- tokens: bfloat16 [2048, 8192], P('dp', 'tensor'), may hold values from -6 to 6
- pattern: int32 [256, 8], P('tensor'), may hold values from 0 to 63, as said below
- first_blocks: bfloat16 [256, 8, 128, 128], P('tensor'), may hold values from -0.1875 to 0.1875
- second_blocks: bfloat16 [256, 8, 128, 128], P('tensor'), may hold values from -0.1875 to 0.1875
- out_grad: bfloat16 [2048, 8192], P('dp', 'tensor'), may hold values from -0.75 to 0.75
Outputs:
- layer_out: bfloat16 [2048, 8192], P('dp', 'tensor')
- input_grad: bfloat16 [2048, 8192], P('dp', 'tensor')
- first_grad: bfloat16 [256, 8, 128, 128], P('tensor')
- second_grad: bfloat16 [256, 8, 128, 128], P('tensor')
Inputs may be any that keep to these rules, and one draw needn't show every extreme that they name: `pattern`: each hidden block row r lists 8 distinct feature blocks: r mod 64, the blocks that differ from it in bit 0, in bit 3 and in the highest bit, and 4 further ones drawn at random. Every feature block is listed by some row.
All inputs are finite; a program needn't handle non-finite values.
Results may differ from a plain program's by a relative error of at most 0.015.
Values may be sent and summed in bfloat16 or wider, within the bound.
A program may use at most 128 MiB of HBM per device.

v0:
```python
import jax
import jax.numpy as jnp
from jax import lax
from jax.sharding import PartitionSpec as P

gelu_scale = 0.7978845608028654
gelu_cube = 0.044715


def gelu_pair(value):
    inner = gelu_scale * (value + gelu_cube * value * value * value)
    tangent = jnp.tanh(inner)
    result = 0.5 * value * (1.0 + tangent)
    slope = 0.5 * (1.0 + tangent) + 0.5 * value * (1.0 - tangent * tangent) * gelu_scale * (
        1.0 + 3.0 * gelu_cube * value * value
    )
    return (result, slope)


def place_blocks(terms, pattern, count):
    targets = jnp.arange(count, dtype=jnp.int32)
    select = (pattern[:, :, None] == targets[None, None, :]).astype(jnp.float32)
    return jnp.einsum("trkc,rkf->ftc", terms, select, precision=lax.Precision.HIGHEST)


def shards(tokens, pattern, first_blocks, second_blocks, out_grad):
    tok_rows = tokens.shape[0]
    block_size = first_blocks.shape[-1]
    group_size = lax.axis_size("tensor")
    feat_blocks = tokens.shape[1] * group_size // block_size
    own_blocks = feat_blocks // group_size
    full_tokens = lax.all_gather(tokens, "tensor", axis=1, tiled=True).reshape(
        tok_rows, feat_blocks, block_size
    )
    picked = full_tokens[:, pattern, :]
    pre = jnp.einsum("trki,rkio->tro", picked, first_blocks, preferred_element_type=jnp.float32)
    value, slope = gelu_pair(pre)
    active = value.astype(jnp.bfloat16)
    contrib = jnp.einsum(
        "tro,rkoc->trkc", active, second_blocks, preferred_element_type=jnp.float32
    )
    out_terms = place_blocks(contrib, pattern, feat_blocks)
    out_rows = lax.psum_scatter(
        out_terms.astype(jnp.bfloat16), "tensor", scatter_dimension=0, tiled=True
    ).astype(jnp.float32)
    layer_out = (
        jnp.transpose(out_rows, (1, 0, 2))
        .reshape(tok_rows, own_blocks * block_size)
        .astype(jnp.bfloat16)
    )
    full_grad = lax.all_gather(out_grad, "tensor", axis=1, tiled=True).reshape(
        tok_rows, feat_blocks, block_size
    )
    grad_picked = full_grad[:, pattern, :]
    second_term = jnp.einsum(
        "tro,trkc->rkoc", active, grad_picked, preferred_element_type=jnp.float32
    )
    act_grad = jnp.einsum(
        "trkc,rkoc->tro", grad_picked, second_blocks, preferred_element_type=jnp.float32
    )
    pre_grad = (act_grad * slope).astype(jnp.bfloat16)
    first_term = jnp.einsum("trki,tro->rkio", picked, pre_grad, preferred_element_type=jnp.float32)
    back_term = jnp.einsum(
        "tro,rkio->trki", pre_grad, first_blocks, preferred_element_type=jnp.float32
    )
    back_terms = place_blocks(back_term, pattern, feat_blocks)
    back_rows = lax.psum_scatter(
        back_terms.astype(jnp.bfloat16), "tensor", scatter_dimension=0, tiled=True
    ).astype(jnp.float32)
    input_grad = (
        jnp.transpose(back_rows, (1, 0, 2))
        .reshape(tok_rows, own_blocks * block_size)
        .astype(jnp.bfloat16)
    )
    first_total, second_total = (
        lax.psum(first_term.astype(jnp.bfloat16), "dp").astype(jnp.float32),
        lax.psum(second_term.astype(jnp.bfloat16), "dp").astype(jnp.float32),
    )
    first_grad = first_total.astype(jnp.bfloat16)
    second_grad = second_total.astype(jnp.bfloat16)
    return (layer_out, input_grad, first_grad, second_grad)


def solution(mesh):
    placed = (
        P("dp", "tensor"),
        P("tensor", None),
        P("tensor", None, None, None),
        P("tensor", None, None, None),
        P("dp", "tensor"),
    )
    return jax.shard_map(
        shards,
        mesh=mesh,
        in_specs=placed,
        out_specs=(
            P("dp", "tensor"),
            P("dp", "tensor"),
            P("tensor", None, None, None),
            P("tensor", None, None, None),
        ),
        check_vma=False,
    )
```

profile of v0, /device:TPU:16, one launch (start us, length us, event | category | flops | bytes accessed | tf_op | source)
XLA Modules:
  0.0 757.9 jit_solution(4094566455043544429)
XLA Ops:
  7.2 1.8 copy.48
  9.1 1.7 copy.55
  11.6 84.0 %all-gather.3.cloned.1.call-done = bf16[256,8192]{0,1:T(8,128)(2,1)} async-done(((bf16[256,256]{0,1:T(8,128)(2,1)}), bf16[256,8192]{0,1:T(8,128)(2,1)}) %all-gather.3.cloned.1.call-update) | async-done | bytes 4194320 | tf_op jit(solution)/shard_map/all_gather | solution.py:32
  95.7 6.4 copy.49
  102.1 75.3 %all-gather.5.cloned.1.call-done = bf16[256,8192]{0,1:T(8,128)(2,1)} async-done(((bf16[256,256]{0,1:T(8,128)(2,1)}), bf16[256,8192]{0,1:T(8,128)(2,1)}) %all-gather.5.cloned.1.call-update) | async-done | bytes 4194320 | tf_op jit(solution)/shard_map/all_gather | solution.py:51
  177.4 6.4 copy.56
  183.7 5.2 gather_fusion
  189.0 5.2 gather_fusion.1
  194.2 6.4 copy.57
  200.7 6.5 copy.50
  207.1 4.2 convolution_bitcast_fusion.3
  211.4 2.6 convert_bitcast_fusion
  214.0 1.3 fusion.19
  216.2 2.6 fusion.12
  220.4 12.1 %bitcast_convert_fusion.1 = bf16[64,256,128]{2,0,1:T(8,128)(2,1)S(1)} fusion(f32[256,8,8,128]{3,0,2,1:T(8,128)S(1)} %convolution_bitcast_fusion.1, s32[8,8]{0,1:T(8,128)S(1)} %copy.47), kind=kOutput, calls=%fused_computation.3 | convolution fusion | flops 1612713984 | bytes 12583168 | tf_op jit(solution)/shard_map/trkc,rkf->ftc/dot_general | solution.py:23
  232.5 4.7 copy.53
  237.5 1.3 copy-done.5
  240.2 12.1 %bitcast_convert_fusion = bf16[64,256,128]{2,0,1:T(8,128)(2,1)S(1)} fusion(f32[256,8,8,128]{3,0,2,1:T(8,128)S(1)} %convolution_bitcast_fusion, s32[8,8]{0,1:T(8,128)S(1)} %copy.47), kind=kOutput, calls=%fused_computation.2 | convolution fusion | flops 1612713984 | bytes 12583168 | tf_op jit(solution)/shard_map/trkc,rkf->ftc/dot_general | solution.py:23
  252.3 4.7 copy.60
  257.0 32.0 %all-reduce.3.cloned.1.call-done = (bf16[8,8,128,128]{3,2,1,0:T(8,128)(2,1)}, bf16[8,8,128,128]{2,3,1,0:T(8,128)(2,1)}) async-done(((bf16[8,8,128,128]{3,2,1,0:T(8,128)(2,1)}, bf16[8,8,128,128]{2,3,1,0:T(8,128)(2,1)}), (bf16[8,8,128,128]{3,2,1,0:T(8,128)(2,1)}, bf16[8,8,128,128]{2,3,1,0:T(8,128)(2,1)})) %all-reduce.3.cloned.1.call-update) | async-done | bytes 4194320 | tf_op jit(solution)/shard_map/psum | solution.py:76
  289.0 4.1 copy.64
  293.1 227.8 %reduce-scatter.3.cloned.1.call-done = bf16[2,256,128]{2,1,0:T(8,128)(2,1)} async-done(((bf16[64,256,128]{2,1,0:T(8,128)(2,1)}), bf16[2,256,128]{2,1,0:T(8,128)(2,1)}) %reduce-scatter.3.cloned.1.call-update) | async-done | bytes 131088 | tf_op jit(solution)/shard_map/reduce_scatter | solution.py:43
  522.6 223.8 %reduce-scatter.5.cloned.1.call-done = bf16[2,256,128]{2,1,0:T(8,128)(2,1)} async-done(((bf16[64,256,128]{2,1,0:T(8,128)(2,1)}), bf16[2,256,128]{2,1,0:T(8,128)(2,1)}) %reduce-scatter.5.cloned.1.call-update) | async-done | bytes 131088 | tf_op jit(solution)/shard_map/reduce_scatter | solution.py:67
  748.2 3.2 copy.87
  (37 shorter events, 8.6 us)
Async XLA Ops:
  7.2 206.9 %copy-start = (bf16[8,8,128,128]{3,2,1,0:T(8,128)(2,1)S(1)}, bf16[8,8,128,128]{3,2,1,0:T(8,128)(2,1)}, u32[]{:S(2)}) copy-start(bf16[8,8,128,128]{3,2,1,0:T(8,128)(2,1)} %param.8) | copy-start | bytes 6291460
  7.2 88.5 %all-gather.3.cloned.1.call-start = ((), (), s32[]{:S(2)}) async-start(), calls=%async_computation.2 | async-start | bytes 4325376 | tf_op jit(solution)/shard_map/all_gather | solution.py:32
  9.1 168.3 %all-gather.5.cloned.1.call-start = ((), (), s32[]{:S(2)}) async-start(), calls=%async_computation.4 | async-start | bytes 4325376 | tf_op jit(solution)/shard_map/all_gather | solution.py:51
  10.8 278.2 %all-reduce.3.cloned.1.call-start = ((), (), s32[]{:S(2)}) async-start(), calls=%async_computation.6 | async-start | bytes 8388608 | tf_op jit(solution)/shard_map/psum | solution.py:76
  207.1 4.3 copy-start.4
  211.4 2.7 copy-start.2
  214.0 2.2 copy-start.3
  215.3 0.8 copy-start.6
  216.2 2.8 copy-start.8
  218.8 302.0 %reduce-scatter.3.cloned.1.call-start = ((), (), s32[]{:S(2)}) async-start(), calls=%async_computation.3 | async-start | bytes 4325376 | tf_op jit(solution)/shard_map/reduce_scatter | solution.py:43
  237.2 1.6 copy-start.5
  237.2 1.7 copy-start.7
  237.2 509.2 %reduce-scatter.5.cloned.1.call-start = ((), (), s32[]{:S(2)}) async-start(), calls=%async_computation.5 | async-start | bytes 4325376 | tf_op jit(solution)/shard_map/reduce_scatter | solution.py:67
  289.0 462.3 %copy-start.1 = (bf16[8,8,128,128]{3,2,1,0:T(8,128)(2,1)S(1)}, bf16[8,8,128,128]{3,2,1,0:T(8,128)(2,1)}, u32[]{:S(2)}) copy-start(bf16[8,8,128,128]{3,2,1,0:T(8,128)(2,1)} %param.8) | copy-start | bytes 6291460
Sparse Core Ops, SparseCore 0:
  11.2 84.4 all-gather.2
  98.8 78.4 all-gather.4
  218.9 70.0 all-reduce.2
  292.7 228.0 reduce-scatter.2
  524.6 221.7 reduce-scatter.4
where the time goes:
time: 759 us; the launch traced here: 758 us
  waiting for transfers between devices  643 us (85%)
  local copies, waits for them, and re-layouts  62.2 us (8%)
  matrix products  37.5 us (5%)
  between operations  13.9 us (2%)
    reduce_scatter x1, waiting for transfers between devices, shards(): lax.psum_scatter(out_terms.astype(jnp.bfloat16), 'tensor', scatter_dimens...  228 us
    reduce_scatter x1, waiting for transfers between devices, shards(): lax.psum_scatter(back_terms.astype(jnp.bfloat16), 'tensor', scatter_dimen...  224 us
    all_gather x1, waiting for transfers between devices, shards(): lax.all_gather(tokens, 'tensor', axis=1, tiled=True)  84 us
    all_gather x1, waiting for transfers between devices, shards(): lax.all_gather(out_grad, 'tensor', axis=1, tiled=True)  75.3 us
    psum x1, waiting for transfers between devices, shards(): lax.psum(first_term.astype(jnp.bfloat16), 'dp').astype(jnp.float32)  32 us
    dot_general x2, matrix products, place_blocks(): jnp.einsum('trkc,rkf->ftc', terms, select, precision=lax.Precision.HIGHEST)  24.3 us
  transfers between devices with their start and end apart: 5, of which 5 were waited for; matrix products, arithmetic and copies ran while one was open for 7% of the time, Pallas kernels for 0%

commit v1 on v0

--- a/solution.py
+++ b/solution.py
@@ -73,7 +73,7 @@
         .astype(jnp.bfloat16)
     )
     first_total, second_total = (
-        lax.psum(first_term.astype(jnp.bfloat16), "dp").astype(jnp.float32),
+        jnp.sum(lax.all_gather(first_term.astype(jnp.bfloat16), "dp"), axis=0).astype(jnp.float32),
         lax.psum(second_term.astype(jnp.bfloat16), "dp").astype(jnp.float32),
     )
     first_grad = first_total.astype(jnp.bfloat16)

time: 759 us -> 836 us (1.10)
  waiting for transfers between devices: 643 us -> 706 us
  other arithmetic: 0.7 us -> 11.6 us
    all_gather x0 -> x1, waiting for transfers between devices: none -> 85.4 us  [shards(): lax.all_gather(first_term.astype(jnp.bfloat16), 'dp')]
    psum x1, waiting for transfers between devices: 32 us -> 10.7 us  [shards(): lax.psum(second_term.astype(jnp.bfloat16), 'dp').astype(jnp.float32)]
    reduce_sum x0 -> x1, other arithmetic: none -> 10.9 us  [shards(): jnp.sum(lax.all_gather(first_term.astype(jnp.bfloat16), 'dp'), axis=0)]
  transfers between devices with their start and end apart: 5 -> 6, of which waited for: 5 -> 6; matrix products, arithmetic and copies ran while one was open for 7% -> 8% of each run, Pallas kernels for 0% -> 0%
where the time goes in v1:
time: 836 us; the launch traced here: 833 us
  waiting for transfers between devices  706 us (84%)
  local copies, waits for them, and re-layouts  58.2 us (7%)
  matrix products  42.1 us (5%)
  between operations  14.2 us (2%)
  other arithmetic  11.6 us (1%)
    reduce_scatter x1, waiting for transfers between devices, shards(): lax.psum_scatter(out_terms.astype(jnp.bfloat16), 'tensor', scatter_dimens...  227 us
    reduce_scatter x1, waiting for transfers between devices, shards(): lax.psum_scatter(back_terms.astype(jnp.bfloat16), 'tensor', scatter_dimen...  224 us
    all_gather x1, waiting for transfers between devices, shards(): lax.all_gather(first_term.astype(jnp.bfloat16), 'dp')  85.4 us
    all_gather x1, waiting for transfers between devices, shards(): lax.all_gather(tokens, 'tensor', axis=1, tiled=True)  83.3 us
    all_gather x1, waiting for transfers between devices, shards(): lax.all_gather(out_grad, 'tensor', axis=1, tiled=True)  75.3 us
    dot_general x2, matrix products, place_blocks(): jnp.einsum('trkc,rkf->ftc', terms, select, precision=lax.Precision.HIGHEST)  24.3 us
  transfers between devices with their start and end apart: 6, of which 6 were waited for; matrix products, arithmetic and copies ran while one was open for 8% of the time, Pallas kernels for 0%

profile of v1, /device:TPU:16, one launch (start us, length us, event | category | flops | bytes accessed | tf_op | source)
XLA Modules:
  0.0 832.9 jit_solution(7958425709193170406)
XLA Ops:
  7.2 1.8 copy.48
  9.1 1.7 copy.55
  12.4 83.3 %all-gather.5.cloned.1.call-done = bf16[256,8192]{0,1:T(8,128)(2,1)} async-done(((bf16[256,256]{0,1:T(8,128)(2,1)}), bf16[256,8192]{0,1:T(8,128)(2,1)}) %all-gather.5.cloned.1.call-update) | async-done | bytes 4194320 | tf_op jit(solution)/shard_map/all_gather | solution.py:32
  95.7 6.4 copy.49
  102.1 75.3 %all-gather.7.cloned.1.call-done = bf16[256,8192]{0,1:T(8,128)(2,1)} async-done(((bf16[256,256]{0,1:T(8,128)(2,1)}), bf16[256,8192]{0,1:T(8,128)(2,1)}) %all-gather.7.cloned.1.call-update) | async-done | bytes 4194320 | tf_op jit(solution)/shard_map/all_gather | solution.py:51
  177.4 6.4 copy.56
  183.7 5.2 gather_fusion
  189.0 5.2 gather_fusion.1
  194.2 6.5 copy.57
  200.7 4.2 convolution_bitcast_fusion.3
  204.9 2.6 convert_bitcast_fusion
  209.1 12.1 %bitcast_convert_fusion.1 = bf16[64,256,128]{2,0,1:T(8,128)(2,1)S(1)} fusion(f32[256,8,8,128]{3,0,2,1:T(8,128)S(1)} %convolution_bitcast_fusion.1, s32[8,8]{0,1:T(8,128)S(1)} %copy.47), kind=kOutput, calls=%fused_computation.3 | convolution fusion | flops 1612713984 | bytes 12583168 | tf_op jit(solution)/shard_map/trkc,rkf->ftc/dot_general | solution.py:23
  221.2 4.6 copy.53
  226.2 3.7 fusion.19
  231.9 12.1 %bitcast_convert_fusion = bf16[64,256,128]{2,0,1:T(8,128)(2,1)S(1)} fusion(f32[256,8,8,128]{3,0,2,1:T(8,128)S(1)} %convolution_bitcast_fusion, s32[8,8]{0,1:T(8,128)S(1)} %copy.47), kind=kOutput, calls=%fused_computation.2 | convolution fusion | flops 1612713984 | bytes 12583168 | tf_op jit(solution)/shard_map/trkc,rkf->ftc/dot_general | solution.py:23
  244.1 4.7 copy.60
  249.1 6.6 copy.50
  255.7 4.8 fusion.12
  260.5 10.7 %all-reduce.2.cloned.1.call-done = bf16[8,8,128,128]{2,3,1,0:T(8,128)(2,1)} async-done(((bf16[8,8,128,128]{2,3,1,0:T(8,128)(2,1)}), bf16[8,8,128,128]{2,3,1,0:T(8,128)(2,1)}) %all-reduce.2.cloned.1.call-update) | async-done | bytes 2097168 | tf_op jit(solution)/shard_map/psum | solution.py:77
  271.2 3.9 copy.64
  275.1 227.4 %reduce-scatter.3.cloned.1.call-done = bf16[2,256,128]{2,1,0:T(8,128)(2,1)} async-done(((bf16[64,256,128]{2,1,0:T(8,128)(2,1)}), bf16[2,256,128]{2,1,0:T(8,128)(2,1)}) %reduce-scatter.3.cloned.1.call-update) | async-done | bytes 131088 | tf_op jit(solution)/shard_map/reduce_scatter | solution.py:43
  504.3 223.7 %reduce-scatter.5.cloned.1.call-done = bf16[2,256,128]{2,1,0:T(8,128)(2,1)} async-done(((bf16[64,256,128]{2,1,0:T(8,128)(2,1)}), bf16[2,256,128]{2,1,0:T(8,128)(2,1)}) %reduce-scatter.5.cloned.1.call-update) | async-done | bytes 131088 | tf_op jit(solution)/shard_map/reduce_scatter | solution.py:67
  729.8 85.4 %all-gather.9.cloned.1.call-done = bf16[64,8,128,128]{3,2,1,0:T(8,128)(2,1)} async-done(((bf16[8,8,128,128]{3,2,1,0:T(8,128)(2,1)}), bf16[64,8,128,128]{3,2,1,0:T(8,128)(2,1)}) %all-gather.9.cloned.1.call-update) | async-done | bytes 16777232 | tf_op jit(solution)/shard_map/all_gather | solution.py:76
  815.2 10.9 %reduce_sum.12 = bf16[8,8,128,128]{3,2,1,0:T(8,128)(2,1)} reduce(bf16[8,8,8,128,128]{4,3,2,1,0:T(8,128)(2,1)} %bitcast.76, bf16[]{:T(256)} %constant.16.clone.1), dimensions={0}, to_apply=%region_2.0 | reduce | flops 7340032 | bytes 18874370 | tf_op jit(solution)/shard_map/reduce_sum | solution.py:76
  (34 shorter events, 9.4 us)
Async XLA Ops:
  7.2 200.7 %copy-start = (bf16[8,8,128,128]{3,2,1,0:T(8,128)(2,1)S(1)}, bf16[8,8,128,128]{3,2,1,0:T(8,128)(2,1)}, u32[]{:S(2)}) copy-start(bf16[8,8,128,128]{3,2,1,0:T(8,128)(2,1)} %param.8) | copy-start | bytes 6291460
  7.2 88.5 %all-gather.5.cloned.1.call-start = ((), (), s32[]{:S(2)}) async-start(), calls=%async_computation.2 | async-start | bytes 4325376 | tf_op jit(solution)/shard_map/all_gather | solution.py:32
  9.1 168.3 %all-gather.7.cloned.1.call-start = ((), (), s32[]{:S(2)}) async-start(), calls=%async_computation.4 | async-start | bytes 4325376 | tf_op jit(solution)/shard_map/all_gather | solution.py:51
  10.8 260.4 %all-reduce.2.cloned.1.call-start = ((), (), s32[]{:S(2)}) async-start(), calls=%async_computation.6 | async-start | bytes 4194304 | tf_op jit(solution)/shard_map/psum | solution.py:77
  200.7 4.3 copy-start.2
  207.6 294.9 %reduce-scatter.3.cloned.1.call-start = ((), (), s32[]{:S(2)}) async-start(), calls=%async_computation.3 | async-start | bytes 4325376 | tf_op jit(solution)/shard_map/reduce_scatter | solution.py:43
  225.9 502.1 %reduce-scatter.5.cloned.1.call-start = ((), (), s32[]{:S(2)}) async-start(), calls=%async_computation.5 | async-start | bytes 4325376 | tf_op jit(solution)/shard_map/reduce_scatter | solution.py:67
  226.2 4.5 copy-start.3
  229.8 0.8 copy-start.4
  248.7 566.4 %all-gather.9.cloned.1.call-start = ((), (), s32[]{:S(2)}) async-start(), calls=%async_computation.7 | async-start | bytes 18874368 | tf_op jit(solution)/shard_map/all_gather | solution.py:76
  249.1 6.6 copy-start.5
  815.2 10.9 %copy-start.1 = (bf16[8,8,128,128]{3,2,1,0:T(8,128)(2,1)S(1)}, bf16[8,8,128,128]{3,2,1,0:T(8,128)(2,1)}, u32[]{:S(2)}) copy-start(bf16[8,8,128,128]{3,2,1,0:T(8,128)(2,1)} %param.8) | copy-start | bytes 6291460
Sparse Core Ops, SparseCore 0:
  11.2 84.4 all-gather.4
  98.8 78.4 all-gather.6
  207.7 63.4 all-reduce.1
  275.0 227.4 reduce-scatter.2
  506.2 221.7 reduce-scatter.4
  730.3 84.7 all-gather.8

commit v2 on v0

--- a/solution.py
+++ b/solution.py
@@ -29,9 +29,9 @@
     group_size = lax.axis_size("tensor")
     feat_blocks = tokens.shape[1] * group_size // block_size
     own_blocks = feat_blocks // group_size
-    full_tokens = lax.all_gather(tokens, "tensor", axis=1, tiled=True).reshape(
-        tok_rows, feat_blocks, block_size
-    )
+    full_tokens = jnp.concatenate(
+        lax.all_to_all(jnp.stack([tokens] * lax.axis_size("tensor")), "tensor", 0, 0), axis=1
+    ).reshape(tok_rows, feat_blocks, block_size)
     picked = full_tokens[:, pattern, :]
     pre = jnp.einsum("trki,rkio->tro", picked, first_blocks, preferred_element_type=jnp.float32)
     value, slope = gelu_pair(pre)

time: 759 us -> 733 us (0.966)
  waiting for transfers between devices: 643 us -> 604 us
  starting transfers between devices: 0.61 us -> 12.1 us
    all_gather x1 -> x0, waiting for transfers between devices: 84 us -> none  [shards(): lax.all_gather(tokens, 'tensor', axis=1, tiled=True)]
    all_gather x1, waiting for transfers between devices: 75.3 us -> 118 us  [shards(): lax.all_gather(out_grad, 'tensor', axis=1, tiled=True)]
    all_to_all x0 -> x1, starting transfers between devices: none -> 11.6 us  [shards(): lax.all_to_all(jnp.stack([tokens] * lax.axis_size('tensor')), 'tensor', 0...]
    another operation x0 -> x2, local copies, waits for them, and re-layouts: none -> 8.79 us  [the longest x1 6.38 us: shards(): full_tokens = jnp.concatenate(lax.all_to_all(jnp.stack([tokens] * lax.axi...]
  transfers between devices with their start and end apart: 5 -> 5, of which waited for: 5 -> 4; matrix products, arithmetic and copies ran while one was open for 7% -> 7% of each run, Pallas kernels for 0% -> 0%
where the time goes in v2:
time: 733 us; the launch traced here: 732 us
  waiting for transfers between devices  604 us (82%)
  local copies, waits for them, and re-layouts  64.1 us (9%)
  matrix products  37.5 us (5%)
  between operations  13.9 us (2%)
  starting transfers between devices  12.1 us (2%)
    reduce_scatter x1, waiting for transfers between devices, shards(): lax.psum_scatter(out_terms.astype(jnp.bfloat16), 'tensor', scatter_dimens...  228 us
    reduce_scatter x1, waiting for transfers between devices, shards(): lax.psum_scatter(back_terms.astype(jnp.bfloat16), 'tensor', scatter_dimen...  224 us
    all_gather x1, waiting for transfers between devices, shards(): lax.all_gather(out_grad, 'tensor', axis=1, tiled=True)  118 us
    psum x1, waiting for transfers between devices, shards(): lax.psum(first_term.astype(jnp.bfloat16), 'dp').astype(jnp.float32)  34 us
    dot_general x2, matrix products, place_blocks(): jnp.einsum('trkc,rkf->ftc', terms, select, precision=lax.Precision.HIGHEST)  24.3 us
  transfers between devices with their start and end apart: 5, of which 4 were waited for; matrix products, arithmetic and copies ran while one was open for 7% of the time, Pallas kernels for 0%

profile of v2, /device:TPU:16, one launch (start us, length us, event | category | flops | bytes accessed | tf_op | source)
XLA Modules:
  0.0 731.7 jit_solution(15221992427890880691)
XLA Ops:
  7.2 1.8 copy.56
  10.1 2.4 stack.2
  12.5 11.6 %all-to-all-start = ((bf16[32,256,256]{1,2,0:T(8,128)(2,1)}), bf16[32,256,256]{1,2,0:T(8,128)(2,1)}, u32[]{:S(2)}, u32[]{:S(2)}) async-start(bf16[32,256,256]{1,2,0:T(8,128)(2,1)} %stack.2), calls=%async_computation | async-start | bytes 8388608 | tf_op jit(solution)/shard_map/all_to_all | solution.py:33
  24.2 118.2 %all-gather.2.cloned.1.call-done = bf16[256,8192]{0,1:T(8,128)(2,1)} async-done(((bf16[256,256]{0,1:T(8,128)(2,1)}), bf16[256,8192]{0,1:T(8,128)(2,1)}) %all-gather.2.cloned.1.call-update) | async-done | bytes 4194320 | tf_op jit(solution)/shard_map/all_gather | solution.py:51
  142.4 6.4 copy.57
  148.8 6.4 copy.50
  155.2 5.2 gather_fusion.1
  160.5 5.2 gather_fusion
  165.7 6.6 copy.51
  172.3 6.5 copy.58
  178.7 4.2 convolution_bitcast_fusion.3
  183.0 2.6 convert_bitcast_fusion
  185.7 1.3 fusion.19
  187.8 2.6 fusion.12
  192.0 12.1 %bitcast_convert_fusion.1 = bf16[64,256,128]{2,0,1:T(8,128)(2,1)S(1)} fusion(f32[256,8,8,128]{3,0,2,1:T(8,128)S(1)} %convolution_bitcast_fusion.1, s32[8,8]{0,1:T(8,128)S(1)} %copy.48), kind=kOutput, calls=%fused_computation.3 | convolution fusion | flops 1612713984 | bytes 12583168 | tf_op jit(solution)/shard_map/trkc,rkf->ftc/dot_general | solution.py:23
  204.1 4.7 copy.54
  209.1 1.3 copy-done.5
  211.8 12.1 %bitcast_convert_fusion = bf16[64,256,128]{2,0,1:T(8,128)(2,1)S(1)} fusion(f32[256,8,8,128]{3,0,2,1:T(8,128)S(1)} %convolution_bitcast_fusion, s32[8,8]{0,1:T(8,128)S(1)} %copy.48), kind=kOutput, calls=%fused_computation.2 | convolution fusion | flops 1612713984 | bytes 12583168 | tf_op jit(solution)/shard_map/trkc,rkf->ftc/dot_general | solution.py:23
  223.9 4.7 copy.61
  228.6 34.0 %all-reduce.3.cloned.1.call-done = (bf16[8,8,128,128]{3,2,1,0:T(8,128)(2,1)}, bf16[8,8,128,128]{2,3,1,0:T(8,128)(2,1)}) async-done(((bf16[8,8,128,128]{3,2,1,0:T(8,128)(2,1)}, bf16[8,8,128,128]{2,3,1,0:T(8,128)(2,1)}), (bf16[8,8,128,128]{3,2,1,0:T(8,128)(2,1)}, bf16[8,8,128,128]{2,3,1,0:T(8,128)(2,1)})) %all-reduce.3.cloned.1.call-update) | async-done | bytes 4194320 | tf_op jit(solution)/shard_map/psum | solution.py:76
  262.7 4.1 copy.65
  266.7 228.0 %reduce-scatter.3.cloned.1.call-done = bf16[2,256,128]{2,1,0:T(8,128)(2,1)} async-done(((bf16[64,256,128]{2,1,0:T(8,128)(2,1)}), bf16[2,256,128]{2,1,0:T(8,128)(2,1)}) %reduce-scatter.3.cloned.1.call-update) | async-done | bytes 131088 | tf_op jit(solution)/shard_map/reduce_scatter | solution.py:43
  496.5 223.7 %reduce-scatter.5.cloned.1.call-done = bf16[2,256,128]{2,1,0:T(8,128)(2,1)} async-done(((bf16[64,256,128]{2,1,0:T(8,128)(2,1)}), bf16[2,256,128]{2,1,0:T(8,128)(2,1)}) %reduce-scatter.5.cloned.1.call-update) | async-done | bytes 131088 | tf_op jit(solution)/shard_map/reduce_scatter | solution.py:67
  722.0 3.2 copy.88
  (37 shorter events, 8.8 us)
Async XLA Ops:
  7.2 178.5 %copy-start = (bf16[8,8,128,128]{3,2,1,0:T(8,128)(2,1)S(1)}, bf16[8,8,128,128]{3,2,1,0:T(8,128)(2,1)}, u32[]{:S(2)}) copy-start(bf16[8,8,128,128]{3,2,1,0:T(8,128)(2,1)} %param.8) | copy-start | bytes 6291460
  7.2 135.2 %all-gather.2.cloned.1.call-start = ((), (), s32[]{:S(2)}) async-start(), calls=%async_computation.4 | async-start | bytes 4325376 | tf_op jit(solution)/shard_map/all_gather | solution.py:51
  12.5 11.6 %copy-start.8 = (s32[8,8]{1,0:T(8,128)S(1)}, s32[8,8]{1,0:T(8,128)}, u32[]{:S(2)}) copy-start(s32[8,8]{1,0:T(8,128)} %param.6) | copy-start | bytes 772
  12.5 136.4 %all-to-all-start = ((bf16[32,256,256]{1,2,0:T(8,128)(2,1)}), bf16[32,256,256]{1,2,0:T(8,128)(2,1)}, u32[]{:S(2)}, u32[]{:S(2)}) async-start(bf16[32,256,256]{1,2,0:T(8,128)(2,1)} %stack.2), calls=%async_computation | async-start | bytes 8388608 | tf_op jit(solution)/shard_map/all_to_all | solution.py:33
  24.1 238.6 %all-reduce.3.cloned.1.call-start = ((), (), s32[]{:S(2)}) async-start(), calls=%async_computation.6 | async-start | bytes 8388608 | tf_op jit(solution)/shard_map/psum | solution.py:76
  178.7 4.3 copy-start.4
  183.0 2.7 copy-start.2
  185.7 2.2 copy-start.3
  187.0 0.8 copy-start.6
  190.4 304.3 %reduce-scatter.3.cloned.1.call-start = ((), (), s32[]{:S(2)}) async-start(), calls=%async_computation.3 | async-start | bytes 4325376 | tf_op jit(solution)/shard_map/reduce_scatter | solution.py:43
  208.8 1.6 copy-start.5
  208.8 1.7 copy-start.7
  208.8 511.4 %reduce-scatter.5.cloned.1.call-start = ((), (), s32[]{:S(2)}) async-start(), calls=%async_computation.5 | async-start | bytes 4325376 | tf_op jit(solution)/shard_map/reduce_scatter | solution.py:67
  262.7 462.5 %copy-start.1 = (bf16[8,8,128,128]{3,2,1,0:T(8,128)(2,1)S(1)}, bf16[8,8,128,128]{3,2,1,0:T(8,128)(2,1)}, u32[]{:S(2)}) copy-start(bf16[8,8,128,128]{3,2,1,0:T(8,128)(2,1)} %param.8) | copy-start | bytes 6291460
Sparse Core Ops, SparseCore 0:
  11.2 131.1 all-gather.1
  190.6 72.0 all-reduce.2
  266.6 228.1 reduce-scatter.2
  498.5 221.6 reduce-scatter.4
